TPU v7x, 256 devices: a whole 4x4x8 slice. The times are simulated.
256 devices in a mesh: pairs: 16 (over z, core), cols: 16 (over y, x).
Axes of the slice: x: 4, y: 4, z: 8, core: 2. Of those that a mesh axis runs over, the one named last changes fastest.
Arguments:
- pair_list: int32 [96, 5], P('pairs'), may hold values from 0 to 15, as said below
- near_tile_block: bfloat16 [96, 2048, 2048], P('pairs', None, 'cols'), may hold values from -0.0546875 to 0.0546875
- history: float32 [4, 32, 32, 2048], P(None, 'pairs', None, 'cols'), may hold values from -6 to 6
- excitation: float32 [4, 32, 32, 2048], P(None, 'pairs', None, 'cols'), may hold values from -6 to 6
- diagonal: float32 [32, 2048], P('pairs', 'cols'), may hold values from 2 to 4
Outputs:
- densities: float32 [4, 32, 32, 2048], P(None, 'pairs', None, 'cols')
Inputs may be any that keep to these rules, and one draw needn't show every extreme that they name: `pair_list`: rows s * 6 to s * 6 + 5 are the slots of index s of pairs. Column 0 and column 2 are below 2, column 1 below 16, column 3 below 4, column 4 is 0 or 1. The live slots of a device come first and number at least 3; among them no value of column 1 appears more than 3 times, and some value exactly 3 times. One device has all 6 slots live.
All inputs are finite; a program needn't handle non-finite values.
Results may differ from a plain program's by a relative error of at most 0.0018.
Values may be sent and summed in bfloat16 or wider, within the bound.
A program may use at most 64 MiB of HBM per device.

v0:
```python
import jax
import jax.numpy as jnp
from jax import lax
from jax.sharding import PartitionSpec as P

SM = 3
STEPS = 4


def shards(pair_list, near_tile_block, history, excitation, diagonal):
    groups = lax.axis_size("pairs")
    delays, clusters, excite, width = history.shape
    buffer_rows = groups * SM
    first_local = pair_list[:, 0]
    owners = pair_list[:, 1]
    second_local = pair_list[:, 2]
    delay_index = pair_list[:, 3]
    live = pair_list[:, 4] == 1
    live_float = live.astype(jnp.float32)
    owner_hits = ((owners[:, None] == jnp.arange(groups)[None, :]) & live[:, None]).astype(
        jnp.int32
    )
    rank = jnp.sum(jnp.cumsum(owner_hits, axis=0) * owner_hits, axis=1) - 1
    position = jnp.where(live, owners * SM + rank, buffer_rows)
    codes = jnp.full((buffer_rows,), -1, jnp.int32)
    codes = codes.at[position].set(delay_index * clusters + second_local, mode="drop")
    wanted = lax.all_to_all(
        codes.reshape(groups, SM), "pairs", split_axis=0, concat_axis=0, tiled=True
    ).reshape(buffer_rows)
    wanted_valid = wanted >= 0
    wanted_index = jnp.maximum(wanted, 0)
    back_table = (
        (wanted_index[None, :] % clusters == jnp.arange(clusters)[:, None]) & wanted_valid[None, :]
    ).astype(jnp.float32)
    first_table = (first_local[None, :] == jnp.arange(clusters)[:, None]).astype(
        jnp.float32
    ) * live_float[None, :]
    slot_source = jnp.minimum(position, buffer_rows - 1)
    own_index = delay_index * clusters + first_local
    results = []
    for step in range(STEPS):
        rounded = history.astype(jnp.bfloat16)
        flat = rounded.reshape(delays * clusters, excite, width)
        outgoing = jnp.where(
            wanted_valid[:, None, None],
            jnp.take(flat, wanted_index, axis=0),
            jnp.zeros((), jnp.bfloat16),
        )
        incoming = lax.all_to_all(
            outgoing.reshape(groups, SM, excite, width),
            "pairs",
            split_axis=0,
            concat_axis=0,
            tiled=True,
        )
        remote = jnp.take(incoming.reshape(buffer_rows, excite, width), slot_source, axis=0)
        forward = jnp.einsum(
            "sek,smk->sem", remote, near_tile_block, preferred_element_type=jnp.float32
        )
        forward_sum = jnp.einsum(
            "cs,sem->cem", first_table, forward, precision=lax.Precision.HIGHEST
        )
        collected = lax.all_gather(rounded, "cols", axis=3, tiled=True)
        near_rows = jnp.take(collected.reshape(delays * clusters, excite, -1), own_index, axis=0)
        backward = jnp.einsum(
            "sem,smk->sek", near_rows, near_tile_block, preferred_element_type=jnp.float32
        )
        backward = backward * live_float[:, None, None]
        outbound = (
            jnp.zeros((buffer_rows, excite, width), jnp.float32)
            .at[position]
            .set(backward, mode="drop")
        )
        received = lax.all_to_all(
            outbound.reshape(groups, SM, excite, width),
            "pairs",
            split_axis=0,
            concat_axis=0,
            tiled=True,
        )
        backward_sum = jnp.einsum(
            "cq,qek->cek",
            back_table,
            received.reshape(buffer_rows, excite, width),
            precision=lax.Precision.HIGHEST,
        )
        total = lax.psum(forward_sum, "cols")
        own_part = lax.dynamic_slice_in_dim(total, lax.axis_index("cols") * width, width, 2)
        field = own_part + backward_sum
        fresh = (excitation[step] - field) / diagonal[:, None, :]
        results.append(fresh)
        history = jnp.concatenate([fresh[None], history[:-1]], axis=0)
    return jnp.stack(results)


def solution(mesh):
    placed = (
        P("pairs", None),
        P("pairs", None, "cols"),
        P(None, "pairs", None, "cols"),
        P(None, "pairs", None, "cols"),
        P("pairs", "cols"),
    )
    return jax.shard_map(
        shards,
        mesh=mesh,
        in_specs=placed,
        out_specs=P(None, "pairs", None, "cols"),
        check_vma=False,
    )
```

profile of v0, /device:TPU:2, one launch (start us, length us, event | category | flops | bytes accessed | tf_op | source)
XLA Modules:
  0.0 696.8 jit_solution(621412180078924286)
XLA Ops:
  11.3 16.0 %all_to_all.49 = s32[16,1,3]{2,1,0:T(1,128)S(1)} all-to-all(s32[16,1,3]{2,1,0:T(1,128)S(1)} %bitcast.106), channel_id=1, replica_groups=mesh['pairs'=16,'cols'=16] {'pairs'}, dimensions={0} | all-to-all | bytes 384 | tf_op jit(solution)/shard_map/all_to_all | solution.py:27
  31.9 3.6 all-to-all-start.1
  37.2 23.3 %all-gather.5.cloned.1.call-done = bf16[4,2,32,2048]{3,2,1,0:T(8,128)(2,1)} async-done(((bf16[4,2,32,128]{3,2,1,0:T(8,128)(2,1)}), bf16[4,2,32,2048]{3,2,1,0:T(8,128)(2,1)}) %all-gather.5.cloned.1.call-update) | async-done | bytes 1048592 | tf_op jit(solution)/shard_map/all_gather | solution.py:63
  60.5 2.8 gather_fusion.2
  69.0 7.2 %all-to-all-start.2 = ((f32[16,3,32,128]{3,2,1,0:T(8,128)}), f32[16,3,32,128]{3,2,1,0:T(8,128)}, u32[]{:S(2)}, u32[]{:S(2)}) async-start(f32[16,3,32,128]{3,2,1,0:T(8,128)} %bitcast.95), calls=%async_computation.2 | async-start | bytes 1572864 | tf_op jit(solution)/shard_map/all_to_all | solution.py:74
  80.9 3.5 fusion.6
  86.1 93.7 %all-reduce.5.cloned.1.call-done = f32[2,32,2048]{2,0,1:T(2,128)} async-done(((f32[2,32,2048]{2,0,1:T(2,128)}), f32[2,32,2048]{2,0,1:T(2,128)}) %all-reduce.5.cloned.1.call-update) | async-done | bytes 524304 | tf_op jit(solution)/shard_map/psum | solution.py:87
  186.2 7.1 %all-to-all-start.3 = ((bf16[16,3,32,128]{3,2,1,0:T(8,128)(2,1)}), bf16[16,3,32,128]{3,2,1,0:T(8,128)(2,1)S(1)}, u32[]{:S(2)}, u32[]{:S(2)}) async-start(bf16[16,3,32,128]{3,2,1,0:T(8,128)(2,1)} %bitcast.17), calls=%async_computation.3 | async-start | bytes 786432 | tf_op jit(solution)/shard_map/all_to_all | solution.py:49
  193.3 37.5 %all-gather.7.cloned.1.call-done = bf16[4,2,32,2048]{3,2,1,0:T(8,128)(2,1)} async-done(((bf16[4,2,32,128]{3,2,1,0:T(8,128)(2,1)}), bf16[4,2,32,2048]{3,2,1,0:T(8,128)(2,1)}) %all-gather.7.cloned.1.call-update) | async-done | bytes 1048592 | tf_op jit(solution)/shard_map/all_gather | solution.py:63
  230.7 2.8 gather_fusion.5
  239.4 7.2 %all-to-all-start.4 = ((f32[16,3,32,128]{3,2,1,0:T(8,128)}), f32[16,3,32,128]{3,2,1,0:T(8,128)}, u32[]{:S(2)}, u32[]{:S(2)}) async-start(f32[16,3,32,128]{3,2,1,0:T(8,128)} %bitcast.96), calls=%async_computation.4 | async-start | bytes 1572864 | tf_op jit(solution)/shard_map/all_to_all | solution.py:74
  250.1 3.5 fusion.4
  253.7 95.3 %all-reduce.7.cloned.1.call-done = f32[2,32,2048]{2,0,1:T(2,128)} async-done(((f32[2,32,2048]{2,0,1:T(2,128)}), f32[2,32,2048]{2,0,1:T(2,128)}) %all-reduce.7.cloned.1.call-update) | async-done | bytes 524304 | tf_op jit(solution)/shard_map/psum | solution.py:87
  355.4 7.1 %all-to-all-start.5 = ((bf16[16,3,32,128]{3,2,1,0:T(8,128)(2,1)}), bf16[16,3,32,128]{3,2,1,0:T(8,128)(2,1)S(1)}, u32[]{:S(2)}, u32[]{:S(2)}) async-start(bf16[16,3,32,128]{3,2,1,0:T(8,128)(2,1)} %bitcast.25), calls=%async_computation.5 | async-start | bytes 786432 | tf_op jit(solution)/shard_map/all_to_all | solution.py:49
  362.5 37.5 %all-gather.9.cloned.1.call-done = bf16[4,2,32,2048]{3,2,1,0:T(8,128)(2,1)} async-done(((bf16[4,2,32,128]{3,2,1,0:T(8,128)(2,1)}), bf16[4,2,32,2048]{3,2,1,0:T(8,128)(2,1)}) %all-gather.9.cloned.1.call-update) | async-done | bytes 1048592 | tf_op jit(solution)/shard_map/all_gather | solution.py:63
  408.6 7.2 %all-to-all-start.6 = ((f32[16,3,32,128]{3,2,1,0:T(8,128)}), f32[16,3,32,128]{3,2,1,0:T(8,128)}, u32[]{:S(2)}, u32[]{:S(2)}) async-start(f32[16,3,32,128]{3,2,1,0:T(8,128)} %bitcast.97), calls=%async_computation.6 | async-start | bytes 1572864 | tf_op jit(solution)/shard_map/all_to_all | solution.py:74
  419.2 3.5 fusion.2
  422.8 95.3 %all-reduce.9.cloned.1.call-done = f32[2,32,2048]{2,0,1:T(2,128)} async-done(((f32[2,32,2048]{2,0,1:T(2,128)}), f32[2,32,2048]{2,0,1:T(2,128)}) %all-reduce.9.cloned.1.call-update) | async-done | bytes 524304 | tf_op jit(solution)/shard_map/psum | solution.py:87
  524.5 7.1 %all-to-all-start.7 = ((bf16[16,3,32,128]{3,2,1,0:T(8,128)(2,1)}), bf16[16,3,32,128]{3,2,1,0:T(8,128)(2,1)S(1)}, u32[]{:S(2)}, u32[]{:S(2)}) async-start(bf16[16,3,32,128]{3,2,1,0:T(8,128)(2,1)} %bitcast.33), calls=%async_computation.7 | async-start | bytes 786432 | tf_op jit(solution)/shard_map/all_to_all | solution.py:49
  531.6 37.5 %all-gather.11.cloned.1.call-done = bf16[4,2,32,2048]{3,2,1,0:T(8,128)(2,1)} async-done(((bf16[4,2,32,128]{3,2,1,0:T(8,128)(2,1)}), bf16[4,2,32,2048]{3,2,1,0:T(8,128)(2,1)}) %all-gather.11.cloned.1.call-update) | async-done | bytes 1048592 | tf_op jit(solution)/shard_map/all_gather | solution.py:63
  569.1 2.8 gather_fusion.11
  577.6 7.2 %all-to-all-start.8 = ((f32[16,3,32,128]{3,2,1,0:T(8,128)}), f32[16,3,32,128]{3,2,1,0:T(8,128)}, u32[]{:S(2)}, u32[]{:S(2)}) async-start(f32[16,3,32,128]{3,2,1,0:T(8,128)} %bitcast.94), calls=%async_computation.8 | async-start | bytes 1572864 | tf_op jit(solution)/shard_map/all_to_all | solution.py:74
  588.4 3.5 fusion
  591.9 95.3 %all-reduce.11.cloned.1.call-done = f32[2,32,2048]{2,0,1:T(2,128)} async-done(((f32[2,32,2048]{2,0,1:T(2,128)}), f32[2,32,2048]{2,0,1:T(2,128)}) %all-reduce.11.cloned.1.call-update) | async-done | bytes 524304 | tf_op jit(solution)/shard_map/psum | solution.py:87
  (179 shorter events, 75.4 us)
Async XLA Ops:
  6.5 54.0 %all-gather.5.cloned.1.call-start = ((), (), s32[]{:S(2)}) async-start(), calls=%async_computation.10 | async-start | bytes 1114112 | tf_op jit(solution)/shard_map/all_gather | solution.py:63
  31.9 37.2 %all-to-all-start.1 = ((bf16[16,3,32,128]{3,2,1,0:T(8,128)(2,1)}), bf16[16,3,32,128]{3,2,1,0:T(8,128)(2,1)S(1)}, u32[]{:S(2)}, u32[]{:S(2)}) async-start(bf16[16,3,32,128]{3,2,1,0:T(8,128)(2,1)} %bitcast.8), calls=%async_computation.1 | async-start | bytes 786432 | tf_op jit(solution)/shard_map/all_to_all | solution.py:49
  69.0 110.7 %all-to-all-start.2 = ((f32[16,3,32,128]{3,2,1,0:T(8,128)}), f32[16,3,32,128]{3,2,1,0:T(8,128)}, u32[]{:S(2)}, u32[]{:S(2)}) async-start(f32[16,3,32,128]{3,2,1,0:T(8,128)} %bitcast.95), calls=%async_computation.2 | async-start | bytes 1572864 | tf_op jit(solution)/shard_map/all_to_all | solution.py:74
  76.2 103.6 %all-reduce.5.cloned.1.call-start = ((), (), s32[]{:S(2)}) async-start(), calls=%async_computation.9 | async-start | bytes 1048576 | tf_op jit(solution)/shard_map/psum | solution.py:87
  84.4 146.3 %all-gather.7.cloned.1.call-start = ((), (), s32[]{:S(2)}) async-start(), calls=%async_computation.12 | async-start | bytes 1114112 | tf_op jit(solution)/shard_map/all_gather | solution.py:63
  186.2 53.2 %all-to-all-start.3 = ((bf16[16,3,32,128]{3,2,1,0:T(8,128)(2,1)}), bf16[16,3,32,128]{3,2,1,0:T(8,128)(2,1)S(1)}, u32[]{:S(2)}, u32[]{:S(2)}) async-start(bf16[16,3,32,128]{3,2,1,0:T(8,128)(2,1)} %bitcast.17), calls=%async_computation.3 | async-start | bytes 786432 | tf_op jit(solution)/shard_map/all_to_all | solution.py:49
  239.4 109.6 %all-to-all-start.4 = ((f32[16,3,32,128]{3,2,1,0:T(8,128)}), f32[16,3,32,128]{3,2,1,0:T(8,128)}, u32[]{:S(2)}, u32[]{:S(2)}) async-start(f32[16,3,32,128]{3,2,1,0:T(8,128)} %bitcast.96), calls=%async_computation.4 | async-start | bytes 1572864 | tf_op jit(solution)/shard_map/all_to_all | solution.py:74
  246.5 102.5 %all-reduce.7.cloned.1.call-start = ((), (), s32[]{:S(2)}) async-start(), calls=%async_computation.11 | async-start | bytes 1048576 | tf_op jit(solution)/shard_map/psum | solution.py:87
  248.1 100.9 %copy-start.13 = (f32[1,2,32,128]{3,2,1,0:T(8,128)S(1)}, f32[1,2,32,128]{3,2,1,0:T(8,128)}, u32[]{:S(2)}) copy-start(f32[1,2,32,128]{3,2,1,0:T(8,128)} %get-tuple-element.17) | copy-start | bytes 98308
  248.1 100.9 %copy-start.24 = (f32[2,128]{1,0:T(2,128)S(1)}, f32[2,128]{1,0:T(2,128)}, u32[]{:S(2)}) copy-start(f32[2,128]{1,0:T(2,128)} %param.15) | copy-start | bytes 3076
  248.1 100.9 %copy-start.34 = (pred[2,48]{1,0:T(4,128)(4,1)S(1)}, pred[2,48]{1,0:T(4,128)(4,1)}, u32[]{:S(2)}) copy-start(pred[2,48]{1,0:T(4,128)(4,1)} %copy-done.33) | copy-start | bytes 292
  253.7 146.3 %all-gather.9.cloned.1.call-start = ((), (), s32[]{:S(2)}) async-start(), calls=%async_computation.14 | async-start | bytes 1114112 | tf_op jit(solution)/shard_map/all_gather | solution.py:63
  355.4 53.2 %all-to-all-start.5 = ((bf16[16,3,32,128]{3,2,1,0:T(8,128)(2,1)}), bf16[16,3,32,128]{3,2,1,0:T(8,128)(2,1)S(1)}, u32[]{:S(2)}, u32[]{:S(2)}) async-start(bf16[16,3,32,128]{3,2,1,0:T(8,128)(2,1)} %bitcast.25), calls=%async_computation.5 | async-start | bytes 786432 | tf_op jit(solution)/shard_map/all_to_all | solution.py:49
  408.6 109.5 %all-to-all-start.6 = ((f32[16,3,32,128]{3,2,1,0:T(8,128)}), f32[16,3,32,128]{3,2,1,0:T(8,128)}, u32[]{:S(2)}, u32[]{:S(2)}) async-start(f32[16,3,32,128]{3,2,1,0:T(8,128)} %bitcast.97), calls=%async_computation.6 | async-start | bytes 1572864 | tf_op jit(solution)/shard_map/all_to_all | solution.py:74
  415.8 102.3 %all-reduce.9.cloned.1.call-start = ((), (), s32[]{:S(2)}) async-start(), calls=%async_computation.13 | async-start | bytes 1048576 | tf_op jit(solution)/shard_map/psum | solution.py:87
  417.1 100.9 %copy-start.12 = (f32[1,2,32,128]{3,2,1,0:T(8,128)S(1)}, f32[1,2,32,128]{3,2,1,0:T(8,128)}, u32[]{:S(2)}) copy-start(f32[1,2,32,128]{3,2,1,0:T(8,128)} %get-tuple-element.16) | copy-start | bytes 98308
  417.1 100.9 %copy-start.25 = (f32[2,128]{1,0:T(2,128)S(1)}, f32[2,128]{1,0:T(2,128)}, u32[]{:S(2)}) copy-start(f32[2,128]{1,0:T(2,128)} %param.15) | copy-start | bytes 3076
  422.7 146.3 %all-gather.11.cloned.1.call-start = ((), (), s32[]{:S(2)}) async-start(), calls=%async_computation.16 | async-start | bytes 1114112 | tf_op jit(solution)/shard_map/all_gather | solution.py:63
  524.5 53.1 %all-to-all-start.7 = ((bf16[16,3,32,128]{3,2,1,0:T(8,128)(2,1)}), bf16[16,3,32,128]{3,2,1,0:T(8,128)(2,1)S(1)}, u32[]{:S(2)}, u32[]{:S(2)}) async-start(bf16[16,3,32,128]{3,2,1,0:T(8,128)(2,1)} %bitcast.33), calls=%async_computation.7 | async-start | bytes 786432 | tf_op jit(solution)/shard_map/all_to_all | solution.py:49
  577.6 109.7 %all-to-all-start.8 = ((f32[16,3,32,128]{3,2,1,0:T(8,128)}), f32[16,3,32,128]{3,2,1,0:T(8,128)}, u32[]{:S(2)}, u32[]{:S(2)}) async-start(f32[16,3,32,128]{3,2,1,0:T(8,128)} %bitcast.94), calls=%async_computation.8 | async-start | bytes 1572864 | tf_op jit(solution)/shard_map/all_to_all | solution.py:74
  584.7 102.5 %all-reduce.11.cloned.1.call-start = ((), (), s32[]{:S(2)}) async-start(), calls=%async_computation.15 | async-start | bytes 1048576 | tf_op jit(solution)/shard_map/psum | solution.py:87
  586.3 100.9 %copy-start.11 = (f32[1,2,32,128]{3,2,1,0:T(8,128)S(1)}, f32[1,2,32,128]{3,2,1,0:T(8,128)}, u32[]{:S(2)}) copy-start(f32[1,2,32,128]{3,2,1,0:T(8,128)} %get-tuple-element.15) | copy-start | bytes 98308
  586.3 100.9 %copy-start.26 = (f32[2,128]{1,0:T(2,128)S(1)}, f32[2,128]{1,0:T(2,128)}, u32[]{:S(2)}) copy-start(f32[2,128]{1,0:T(2,128)} %param.15) | copy-start | bytes 3076
  586.3 100.9 %copy-start.36 = (pred[2,48]{1,0:T(4,128)(4,1)S(1)}, pred[2,48]{1,0:T(4,128)(4,1)}, u32[]{:S(2)}) copy-start(pred[2,48]{1,0:T(4,128)(4,1)} %copy-done.33) | copy-start | bytes 292
  (35 other events, 1218.3 us)
Sparse Core Ops, SparseCore 0:
  9.7 50.7 all-gather.4
  84.5 95.1 all-reduce.4
  183.1 47.6 all-gather.6
  253.8 95.1 all-reduce.6
  352.3 47.6 all-gather.8
  422.8 95.1 all-reduce.8
  521.4 47.6 all-gather.10
  592.0 95.1 all-reduce.10
where the time goes:
time: 699 us; the launch traced here: 697 us
  waiting for transfers between devices  515 us (74%)
  starting transfers between devices  54.3 us (8%)
  local copies, waits for them, and re-layouts  41.9 us (6%)
  matrix products  39.5 us (6%)
  blocking collectives  16 us (2%)
  other arithmetic  15.7 us (2%)
  between operations  14 us (2%)
    psum x4, waiting for transfers between devices, shards(): total = lax.psum(forward_sum, 'cols')  380 us
    all_gather x4, waiting for transfers between devices, shards(): collected = lax.all_gather(rounded, 'cols', axis=3, tiled=True)  136 us
    all_to_all x4, starting transfers between devices, shards(): lax.all_to_all(outbound.reshape(groups, SM, excite, width), 'pairs', spli...  28.7 us
    all_to_all x4, starting transfers between devices, shards(): lax.all_to_all(outgoing.reshape(groups, SM, excite, width), 'pairs', spli...  24.9 us
    all_to_all x1, blocking collectives, shards(): lax.all_to_all(codes.reshape(groups, SM), 'pairs', split_axis=0, concat_a...  16 us
  transfers between devices with their start and end apart: 16, of which 8 were waited for; matrix products, arithmetic and copies ran while one was open for 12% of the time, Pallas kernels for 0%

commit v1 on v0

--- a/solution.py
+++ b/solution.py
@@ -84,7 +84,7 @@
             received.reshape(buffer_rows, excite, width),
             precision=lax.Precision.HIGHEST,
         )
-        total = lax.psum(forward_sum, "cols")
+        total = jnp.sum(lax.all_gather(forward_sum, "cols"), axis=0)
         own_part = lax.dynamic_slice_in_dim(total, lax.axis_index("cols") * width, width, 2)
         field = own_part + backward_sum
         fresh = (excitation[step] - field) / diagonal[:, None, :]

time: 699 us -> 570 us (0.82)
  waiting for transfers between devices: 515 us -> 338 us
  blocking collectives: 16 us -> 61.7 us
  other arithmetic: 15.7 us -> 29.8 us
  starting transfers between devices: 54.3 us -> 41.2 us
    psum x4 -> x0, waiting for transfers between devices: 380 us -> none  [shards(): total = lax.psum(forward_sum, 'cols')]
    all_gather x0 -> x4, waiting for transfers between devices: none -> 251 us  [shards(): total = jnp.sum(lax.all_gather(forward_sum, 'cols'), axis=0)]
    all_gather x4, waiting for transfers between devices: 136 us -> 69.4 us  [shards(): collected = lax.all_gather(rounded, 'cols', axis=3, tiled=True)]
    all_to_all x1 -> x3, blocking collectives: 16 us -> 61.7 us  [shards(): lax.all_to_all(outgoing.reshape(groups, SM, excite, width), 'pairs', spli...]
    all_to_all x4 -> x1, starting transfers between devices: 24.9 us -> 3.55 us  [shards(): lax.all_to_all(outgoing.reshape(groups, SM, excite, width), 'pairs', spli...]
    reduce_sum x0 -> x4, other arithmetic: none -> 18.9 us  [shards(): total = jnp.sum(lax.all_gather(forward_sum, 'cols'), axis=0)]
    all_to_all x4 -> x1, waiting for transfers between devices: 0.01 us -> 12.2 us  [shards(): lax.all_to_all(outgoing.reshape(groups, SM, excite, width), 'pairs', spli...]
    all_to_all x0 -> x1, starting transfers between devices: none -> 8.57 us  [shards(): lax.all_to_all(codes.reshape(groups, SM), 'pairs', split_axis=0, concat_a...]
  transfers between devices with their start and end apart: 16 -> 14, of which waited for: 8 -> 10; matrix products, arithmetic and copies ran while one was open for 12% -> 17% of each run, Pallas kernels for 0% -> 0%
where the time goes in v1:
time: 570 us; the launch traced here: 567 us
  waiting for transfers between devices  338 us (59%)
  blocking collectives  61.7 us (11%)
  local copies, waits for them, and re-layouts  48.3 us (8%)
  starting transfers between devices  41.2 us (7%)
  matrix products  33.6 us (6%)
  other arithmetic  29.8 us (5%)
  between operations  14.2 us (2%)
    all_gather x4, waiting for transfers between devices, shards(): total = jnp.sum(lax.all_gather(forward_sum, 'cols'), axis=0)  251 us
    all_gather x4, waiting for transfers between devices, shards(): collected = lax.all_gather(rounded, 'cols', axis=3, tiled=True)  69.4 us
    all_to_all x3, blocking collectives, shards(): lax.all_to_all(outgoing.reshape(groups, SM, excite, width), 'pairs', spli...  61.7 us
    all_to_all x4, starting transfers between devices, shards(): lax.all_to_all(outbound.reshape(groups, SM, excite, width), 'pairs', spli...  28.5 us
    reduce_sum x4, other arithmetic, shards(): total = jnp.sum(lax.all_gather(forward_sum, 'cols'), axis=0)  18.9 us
    all_to_all x1, waiting for transfers between devices, shards(): lax.all_to_all(outgoing.reshape(groups, SM, excite, width), 'pairs', spli...  12.2 us
  transfers between devices with their start and end apart: 14, of which 10 were waited for; matrix products, arithmetic and copies ran while one was open for 17% of the time, Pallas kernels for 0%

profile of v1, /device:TPU:2, one launch (start us, length us, event | category | flops | bytes accessed | tf_op | source)
XLA Modules:
  0.0 567.0 jit_solution(7948942046672317914)
XLA Ops:
  9.5 8.6 %all-to-all-start = ((s32[16,1,3]{2,1,0:T(1,128)}), s32[16,1,3]{2,1,0:T(1,128)S(1)}, u32[]{:S(2)}, u32[]{:S(2)}) async-start(s32[16,1,3]{2,1,0:T(1,128)} %bitcast.6), calls=%async_computation | async-start | bytes 16384 | tf_op jit(solution)/shard_map/all_to_all | solution.py:27
  19.7 6.0 %all-to-all-done = s32[16,1,3]{2,1,0:T(1,128)S(1)} async-done(((s32[16,1,3]{2,1,0:T(1,128)}), s32[16,1,3]{2,1,0:T(1,128)S(1)}, u32[]{:S(2)}, u32[]{:S(2)}) %all-to-all-start) | async-done | bytes 224 | tf_op jit(solution)/shard_map/all_to_all | solution.py:27
  29.7 3.6 all-to-all-start.1
  34.6 12.2 %all-to-all-done.1 = bf16[16,3,32,128]{3,2,1,0:T(8,128)(2,1)S(1)} async-done(((bf16[16,3,32,128]{3,2,1,0:T(8,128)(2,1)}), bf16[16,3,32,128]{3,2,1,0:T(8,128)(2,1)S(1)}, u32[]{:S(2)}, u32[]{:S(2)}) %all-to-all-start.1) | async-done | bytes 393248 | tf_op jit(solution)/shard_map/all_to_all | solution.py:49
  54.0 16.8 %all-gather.13.cloned.1.call-done = bf16[4,2,32,2048]{3,2,1,0:T(8,128)(2,1)} async-done(((bf16[4,2,32,128]{3,2,1,0:T(8,128)(2,1)}), bf16[4,2,32,2048]{3,2,1,0:T(8,128)(2,1)}) %all-gather.13.cloned.1.call-update) | async-done | bytes 1048592 | tf_op jit(solution)/shard_map/all_gather | solution.py:63
  78.4 7.1 %all-to-all-start.2 = ((f32[16,3,32,128]{3,2,1,0:T(8,128)}), f32[16,3,32,128]{3,2,1,0:T(8,128)}, u32[]{:S(2)}, u32[]{:S(2)}) async-start(f32[16,3,32,128]{3,2,1,0:T(8,128)} %bitcast.103), calls=%async_computation.2 | async-start | bytes 1572864 | tf_op jit(solution)/shard_map/all_to_all | solution.py:74
  87.2 61.6 %all-gather.21.cloned.1.call-done = f32[32,32,2048]{2,1,0:T(8,128)} async-done(((f32[2,32,2048]{2,1,0:T(8,128)}), f32[32,32,2048]{2,1,0:T(8,128)}) %all-gather.21.cloned.1.call-update) | async-done | bytes 8388624 | tf_op jit(solution)/shard_map/all_gather | solution.py:87
  148.8 4.7 reduce_sum.46
  159.9 20.6 %all_to_all.49 = bf16[16,3,32,128]{3,2,1,0:T(8,128)(2,1)S(1)} all-to-all(bf16[16,3,32,128]{3,2,1,0:T(8,128)(2,1)S(1)} %bitcast.107), channel_id=1, replica_groups=mesh['pairs'=16,'cols'=16] {'pairs'}, dimensions={0} | all-to-all | bytes 786432 | tf_op jit(solution)/shard_map/all_to_all | solution.py:49
  187.6 17.6 %all-gather.15.cloned.1.call-done = bf16[4,2,32,2048]{3,2,1,0:T(8,128)(2,1)} async-done(((bf16[4,2,32,128]{3,2,1,0:T(8,128)(2,1)}), bf16[4,2,32,2048]{3,2,1,0:T(8,128)(2,1)}) %all-gather.15.cloned.1.call-update) | async-done | bytes 1048592 | tf_op jit(solution)/shard_map/all_gather | solution.py:63
  205.2 2.9 gather_fusion.5
  212.9 7.1 %all-to-all-start.4 = ((f32[16,3,32,128]{3,2,1,0:T(8,128)}), f32[16,3,32,128]{3,2,1,0:T(8,128)}, u32[]{:S(2)}, u32[]{:S(2)}) async-start(f32[16,3,32,128]{3,2,1,0:T(8,128)} %bitcast.104), calls=%async_computation.4 | async-start | bytes 1572864 | tf_op jit(solution)/shard_map/all_to_all | solution.py:74
  220.1 63.0 %all-gather.23.cloned.1.call-done = f32[32,32,2048]{2,1,0:T(8,128)} async-done(((f32[2,32,2048]{2,1,0:T(8,128)}), f32[32,32,2048]{2,1,0:T(8,128)}) %all-gather.23.cloned.1.call-update) | async-done | bytes 8388624 | tf_op jit(solution)/shard_map/all_gather | solution.py:87
  283.1 4.7 reduce_sum.47
  294.3 20.6 %all_to_all.50 = bf16[16,3,32,128]{3,2,1,0:T(8,128)(2,1)S(1)} all-to-all(bf16[16,3,32,128]{3,2,1,0:T(8,128)(2,1)S(1)} %bitcast.108), channel_id=1, replica_groups=mesh['pairs'=16,'cols'=16] {'pairs'}, dimensions={0} | all-to-all | bytes 786432 | tf_op jit(solution)/shard_map/all_to_all | solution.py:49
  322.0 17.6 %all-gather.17.cloned.1.call-done = bf16[4,2,32,2048]{3,2,1,0:T(8,128)(2,1)} async-done(((bf16[4,2,32,128]{3,2,1,0:T(8,128)(2,1)}), bf16[4,2,32,2048]{3,2,1,0:T(8,128)(2,1)}) %all-gather.17.cloned.1.call-update) | async-done | bytes 1048592 | tf_op jit(solution)/shard_map/all_gather | solution.py:63
  347.3 7.1 %all-to-all-start.6 = ((f32[16,3,32,128]{3,2,1,0:T(8,128)}), f32[16,3,32,128]{3,2,1,0:T(8,128)}, u32[]{:S(2)}, u32[]{:S(2)}) async-start(f32[16,3,32,128]{3,2,1,0:T(8,128)} %bitcast.105), calls=%async_computation.6 | async-start | bytes 1572864 | tf_op jit(solution)/shard_map/all_to_all | solution.py:74
  354.7 62.8 %all-gather.25.cloned.1.call-done = f32[32,32,2048]{2,1,0:T(8,128)} async-done(((f32[2,32,2048]{2,1,0:T(8,128)}), f32[32,32,2048]{2,1,0:T(8,128)}) %all-gather.25.cloned.1.call-update) | async-done | bytes 8388624 | tf_op jit(solution)/shard_map/all_gather | solution.py:87
  417.4 4.7 reduce_sum.48
  428.6 20.6 %all_to_all.51 = bf16[16,3,32,128]{3,2,1,0:T(8,128)(2,1)S(1)} all-to-all(bf16[16,3,32,128]{3,2,1,0:T(8,128)(2,1)S(1)} %bitcast.106), channel_id=1, replica_groups=mesh['pairs'=16,'cols'=16] {'pairs'}, dimensions={0} | all-to-all | bytes 786432 | tf_op jit(solution)/shard_map/all_to_all | solution.py:49
  456.3 17.5 %all-gather.19.cloned.1.call-done = bf16[4,2,32,2048]{3,2,1,0:T(8,128)(2,1)} async-done(((bf16[4,2,32,128]{3,2,1,0:T(8,128)(2,1)}), bf16[4,2,32,2048]{3,2,1,0:T(8,128)(2,1)}) %all-gather.19.cloned.1.call-update) | async-done | bytes 1048592 | tf_op jit(solution)/shard_map/all_gather | solution.py:63
  481.6 7.1 %all-to-all-start.8 = ((f32[16,3,32,128]{3,2,1,0:T(8,128)}), f32[16,3,32,128]{3,2,1,0:T(8,128)}, u32[]{:S(2)}, u32[]{:S(2)}) async-start(f32[16,3,32,128]{3,2,1,0:T(8,128)} %bitcast.102), calls=%async_computation.8 | async-start | bytes 1572864 | tf_op jit(solution)/shard_map/all_to_all | solution.py:74
  488.7 63.2 %all-gather.27.cloned.1.call-done = f32[32,32,2048]{2,1,0:T(8,128)} async-done(((f32[2,32,2048]{2,1,0:T(8,128)}), f32[32,32,2048]{2,1,0:T(8,128)}) %all-gather.27.cloned.1.call-update) | async-done | bytes 8388624 | tf_op jit(solution)/shard_map/all_gather | solution.py:87
  551.9 4.7 reduce_sum.49
  (207 shorter events, 90.7 us)
Async XLA Ops:
  6.5 41.5 %copy-start = (bf16[6,2048,128]{2,1,0:T(8,128)(2,1)S(1)}, bf16[6,2048,128]{2,1,0:T(8,128)(2,1)}, u32[]{:S(2)}) copy-start(bf16[6,2048,128]{2,1,0:T(8,128)(2,1)} %param.12) | copy-start | bytes 9437188
  7.7 46.2 %copy-start.19 = (s32[6]{0:T(128)}, s32[6]{0:T(128)S(1)}, u32[]{:S(2)}) copy-start(s32[6]{0:T(128)S(1)} %get-tuple-element.8) | copy-start | bytes 76
  7.8 65.7 %copy-start.15 = (f32[6]{0:T(128)}, f32[6]{0:T(128)S(1)}, u32[]{:S(2)}) copy-start(f32[6]{0:T(128)S(1)} %get-tuple-element.23) | copy-start | bytes 76
  9.5 16.2 %all-to-all-start = ((s32[16,1,3]{2,1,0:T(1,128)}), s32[16,1,3]{2,1,0:T(1,128)S(1)}, u32[]{:S(2)}, u32[]{:S(2)}) async-start(s32[16,1,3]{2,1,0:T(1,128)} %bitcast.6), calls=%async_computation | async-start | bytes 16384 | tf_op jit(solution)/shard_map/all_to_all | solution.py:27
  18.1 52.7 %all-gather.13.cloned.1.call-start = ((), (), s32[]{:S(2)}) async-start(), calls=%async_computation.9 | async-start | bytes 1114112 | tf_op jit(solution)/shard_map/all_gather | solution.py:63
  26.5 60.6 %copy-start.26 = (pred[48]{0:T(512)(128)(4,1)}, pred[48]{0:T(512)(128)(4,1)S(1)}, u32[]{:S(2)}) copy-start(pred[48]{0:T(512)(128)(4,1)S(1)} %ge.28) | copy-start | bytes 148
  29.7 17.1 %all-to-all-start.1 = ((bf16[16,3,32,128]{3,2,1,0:T(8,128)(2,1)}), bf16[16,3,32,128]{3,2,1,0:T(8,128)(2,1)S(1)}, u32[]{:S(2)}, u32[]{:S(2)}) async-start(bf16[16,3,32,128]{3,2,1,0:T(8,128)(2,1)} %bitcast.8), calls=%async_computation.1 | async-start | bytes 786432 | tf_op jit(solution)/shard_map/all_to_all | solution.py:49
  33.2 115.5 %all-gather.21.cloned.1.call-start = ((), (), s32[]{:S(2)}) async-start(), calls=%async_computation.13 | async-start | bytes 8912896 | tf_op jit(solution)/shard_map/all_gather | solution.py:87
  78.4 75.9 %all-to-all-start.2 = ((f32[16,3,32,128]{3,2,1,0:T(8,128)}), f32[16,3,32,128]{3,2,1,0:T(8,128)}, u32[]{:S(2)}, u32[]{:S(2)}) async-start(f32[16,3,32,128]{3,2,1,0:T(8,128)} %bitcast.103), calls=%async_computation.2 | async-start | bytes 1572864 | tf_op jit(solution)/shard_map/all_to_all | solution.py:74
  85.5 119.7 %all-gather.15.cloned.1.call-start = ((), (), s32[]{:S(2)}) async-start(), calls=%async_computation.10 | async-start | bytes 1114112 | tf_op jit(solution)/shard_map/all_gather | solution.py:63
  86.5 70.3 %copy-start.1 = (bf16[3,2,32,128]{3,2,1,0:T(8,128)(2,1)}, bf16[3,2,32,128]{3,2,1,0:T(8,128)(2,1)S(1)}, u32[]{:S(2)}) copy-start(bf16[3,2,32,128]{3,2,1,0:T(8,128)(2,1)S(1)} %slice.43) | copy-start | bytes 147460
  87.2 67.1 %copy-start.42 = (pred[2,48]{1,0:T(4,128)(4,1)}, pred[2,48]{1,0:T(4,128)(4,1)S(1)}, u32[]{:S(2)}) copy-start(pred[2,48]{1,0:T(4,128)(4,1)S(1)} %compare_and_fusion.3) | copy-start | bytes 292
  157.5 125.6 %all-gather.23.cloned.1.call-start = ((), (), s32[]{:S(2)}) async-start(), calls=%async_computation.14 | async-start | bytes 8912896 | tf_op jit(solution)/shard_map/all_gather | solution.py:87
  212.9 75.7 %all-to-all-start.4 = ((f32[16,3,32,128]{3,2,1,0:T(8,128)}), f32[16,3,32,128]{3,2,1,0:T(8,128)}, u32[]{:S(2)}, u32[]{:S(2)}) async-start(f32[16,3,32,128]{3,2,1,0:T(8,128)} %bitcast.104), calls=%async_computation.4 | async-start | bytes 1572864 | tf_op jit(solution)/shard_map/all_to_all | solution.py:74
  220.1 119.5 %all-gather.17.cloned.1.call-start = ((), (), s32[]{:S(2)}) async-start(), calls=%async_computation.11 | async-start | bytes 1114112 | tf_op jit(solution)/shard_map/all_gather | solution.py:63
  220.1 71.0 %copy-start.3 = (bf16[3,2,32,128]{3,2,1,0:T(8,128)(2,1)}, bf16[3,2,32,128]{3,2,1,0:T(8,128)(2,1)S(1)}, u32[]{:S(2)}) copy-start(bf16[3,2,32,128]{3,2,1,0:T(8,128)(2,1)S(1)} %fusion.39) | copy-start | bytes 147460
  291.8 125.6 %all-gather.25.cloned.1.call-start = ((), (), s32[]{:S(2)}) async-start(), calls=%async_computation.15 | async-start | bytes 8912896 | tf_op jit(solution)/shard_map/all_gather | solution.py:87
  318.1 24.3 %copy-start.36 = (pred[6]{0:T(512)(128)(4,1)S(1)}, pred[6]{0:T(512)(128)(4,1)}, u32[]{:S(2)}) copy-start(pred[6]{0:T(512)(128)(4,1)} %copy-done.34) | copy-start | bytes 22
  347.3 75.7 %all-to-all-start.6 = ((f32[16,3,32,128]{3,2,1,0:T(8,128)}), f32[16,3,32,128]{3,2,1,0:T(8,128)}, u32[]{:S(2)}, u32[]{:S(2)}) async-start(f32[16,3,32,128]{3,2,1,0:T(8,128)} %bitcast.105), calls=%async_computation.6 | async-start | bytes 1572864 | tf_op jit(solution)/shard_map/all_to_all | solution.py:74
  354.4 119.5 %all-gather.19.cloned.1.call-start = ((), (), s32[]{:S(2)}) async-start(), calls=%async_computation.12 | async-start | bytes 1114112 | tf_op jit(solution)/shard_map/all_gather | solution.py:63
  426.1 125.8 %all-gather.27.cloned.1.call-start = ((), (), s32[]{:S(2)}) async-start(), calls=%async_computation.16 | async-start | bytes 8912896 | tf_op jit(solution)/shard_map/all_gather | solution.py:87
  427.8 24.7 %copy-start.18 = (f32[6]{0:T(128)S(1)}, f32[6]{0:T(128)}, u32[]{:S(2)}) copy-start(f32[6]{0:T(128)} %copy-done.15) | copy-start | bytes 76
  427.8 24.7 %copy-start.22 = (s32[6]{0:T(128)S(1)}, s32[6]{0:T(128)}, u32[]{:S(2)}) copy-start(s32[6]{0:T(128)} %copy-done.19) | copy-start | bytes 76
  481.6 75.9 %all-to-all-start.8 = ((f32[16,3,32,128]{3,2,1,0:T(8,128)}), f32[16,3,32,128]{3,2,1,0:T(8,128)}, u32[]{:S(2)}, u32[]{:S(2)}) async-start(f32[16,3,32,128]{3,2,1,0:T(8,128)} %bitcast.102), calls=%async_computation.8 | async-start | bytes 1572864 | tf_op jit(solution)/shard_map/all_to_all | solution.py:74
  (42 other events, 352.3 us)
Sparse Core Ops, SparseCore 0:
  21.3 49.4 all-gather.12
  73.2 75.5 all-gather.20
  157.6 47.5 all-gather.14
  207.5 75.5 all-gather.22
  291.9 47.5 all-gather.16
  341.8 75.5 all-gather.24
  426.3 47.5 all-gather.18
  476.3 75.5 all-gather.26
